TPU v7x, 32 devices: a whole 2x2x4 slice. The times are simulated.
32 devices in a mesh: kv: 2 (over y), ctx: 16 (over z, x, core).
Axes of the slice: x: 2, y: 2, z: 4, core: 2. Of those that a mesh axis runs over, the one named last changes fastest.
Arguments:
- residual: bfloat16 [64, 8192], P(None, 'ctx'), may hold values from -8 to 8
- queries: bfloat16 [64, 8192], P(None, 'kv'), may hold values from -16 to 16
- draft_token_keys: bfloat16 [64, 1024], P(None, 'kv'), may hold values from -32 to 32
- draft_token_values: bfloat16 [64, 1024], P(None, 'kv'), may hold values from -8 to 8
- cache_keys: bfloat16 [2, 8192, 1024], P(None, 'ctx', 'kv'), may hold values from -32 to 32
- cached_value_rows: bfloat16 [2, 8192, 1024], P(None, 'ctx', 'kv'), may hold values from -8 to 8
- tenant_ids: int32 [64], replicated, may hold values from 0 to 1, as said below
- tree_mask: int32 [64, 64], replicated, may hold values from 0 to 1, as said below
- cache_lengths: int32 [2], replicated, may hold values from 4097 to 8192
- out_weight: bfloat16 [8192, 8192], P('kv', 'ctx'), may hold values from -0.0625 to 0.0625
- out_signs: bfloat16 [2, 8192, 8192], P(None, 'kv', 'ctx'), may hold values from -1 to 1, as said below
- norm_gain: float32 [8192], P('ctx'), may hold values from 0.1 to 1.9
- gate_weight: bfloat16 [8192, 16384], P(None, ('kv', 'ctx')), may hold values from -0.0625 to 0.0625
- up_weight: bfloat16 [8192, 16384], P(None, ('kv', 'ctx')), may hold values from -0.0625 to 0.0625
- down_weight: bfloat16 [16384, 8192], P(('kv', 'ctx')), may hold values from -0.09375 to 0.09375
- gate_signs: bfloat16 [2, 8192, 16384], P(None, None, ('kv', 'ctx')), may hold values from -1 to 1, as said below
- up_signs: bfloat16 [2, 8192, 16384], P(None, None, ('kv', 'ctx')), may hold values from -1 to 1, as said below
- down_signs: bfloat16 [2, 16384, 8192], P(None, ('kv', 'ctx')), may hold values from -1 to 1, as said below
- delta_scale: float32 [2, 4], replicated, may hold values from 0.3 to 0.9
Outputs:
- mixed: bfloat16 [64, 8192], P(None, 'ctx')
Inputs may be any that keep to these rules, and one draw needn't show every extreme that they name: `tenant_ids`: exactly 32 tokens belong to each tenant. `tree_mask`: entry (i, j) is 1 exactly when token j is token i or an ancestor of token i in the draft tree of their common tenant; each tenant's 32 tokens form one tree. `out_signs`: every entry is 1 or -1. `gate_signs`: every entry is 1 or -1. `up_signs`: every entry is 1 or -1. `down_signs`: every entry is 1 or -1.
All inputs are finite; a program needn't handle non-finite values.
Results may differ from a plain program's by a relative error of at most 0.013.
Values may be sent and summed in bfloat16 or wider, within the bound.
No kernel may reach another device: no remote copies, remote signals or barrier semaphores. Data moves between devices by JAX's collectives and lax.ppermute only.
A program may use at most 192 MiB of HBM per device.

v0:
```python
import jax
import jax.numpy as jnp
from jax import lax
from jax.sharding import PartitionSpec as P

D = 8192
QUERY_HEADS = 64
HEAD_SIZE = 128
FF = 16384
NEG = -1e30
EPS = 1e-05


def combine(first, second):
    first_top, first_total, first_out = first
    second_top, second_total, second_out = second
    peak = jnp.maximum(first_top, second_top)
    first_scale = jnp.exp(first_top - peak)
    second_scale = jnp.exp(second_top - peak)
    total = first_total * first_scale + second_total * second_scale
    merged = first_out * first_scale[..., None] + second_out * second_scale[..., None]
    return (peak, total, merged)


def draft_rows(query_rows, group_rows, visible_rows, key_rows, value_rows, factor):
    groups = key_rows.shape[1]
    choose = (group_rows[:, None] == jnp.arange(groups, dtype=jnp.int32)[None, :]).astype(
        jnp.float32
    )
    every_group = (
        jnp.einsum("rd,kgd->rgk", query_rows, key_rows, preferred_element_type=jnp.float32) * factor
    )
    scores = jnp.einsum("rgk,rg->rk", every_group, choose, precision=lax.Precision.HIGHEST)
    masked = jnp.where(visible_rows, scores, NEG)
    peak = jnp.max(masked, axis=-1)
    weights = jnp.where(visible_rows, jnp.exp(masked - peak[:, None]), 0.0)
    total = jnp.sum(weights, axis=-1)
    every_value = jnp.einsum(
        "rk,kgd->rgd", weights.astype(jnp.bfloat16), value_rows, preferred_element_type=jnp.float32
    )
    result = jnp.einsum("rgd,rg->rd", every_value, choose, precision=lax.Precision.HIGHEST)
    return (peak, total, result)


def shards(
    residual,
    queries,
    draft_token_keys,
    draft_token_values,
    cache_keys,
    cached_value_rows,
    tenant_ids,
    tree_mask,
    cache_lengths,
    out_weight,
    out_signs,
    norm_gain,
    gate_weight,
    up_weight,
    down_weight,
    gate_signs,
    up_signs,
    down_signs,
    delta_scale,
):
    tenants = cache_keys.shape[0]
    tokens = tenant_ids.shape[0]
    draft = tokens // tenants
    heads_here = queries.shape[1] // HEAD_SIZE
    groups_here = draft_token_keys.shape[1] // HEAD_SIZE
    group_width = heads_here // groups_here
    ctx_rows = cache_keys.shape[1]
    factor = HEAD_SIZE ** (-0.5)
    sort_order = jnp.argsort(tenant_ids, stable=True)
    inverse = jnp.argsort(sort_order)
    sorted_queries = queries[sort_order]
    query_blocks = sorted_queries.reshape(tenants, draft, groups_here, group_width, HEAD_SIZE)
    draft_key_lines = draft_token_keys[sort_order].reshape(tokens, groups_here, HEAD_SIZE)
    draft_value_lines = draft_token_values[sort_order].reshape(tokens, groups_here, HEAD_SIZE)
    visible = tree_mask[sort_order][:, sort_order] > 0
    first_slot = lax.axis_index("ctx") * ctx_rows
    slot_ids = first_slot + jnp.arange(ctx_rows, dtype=jnp.int32)
    live = (slot_ids[None, :] < cache_lengths[:, None])[:, None, None, None, :]
    cache_key_blocks = cache_keys.reshape(tenants, ctx_rows, groups_here, HEAD_SIZE)
    cache_value_blocks = cached_value_rows.reshape(tenants, ctx_rows, groups_here, HEAD_SIZE)
    scores = (
        jnp.einsum(
            "tqgwd,tjgd->tqgwj", query_blocks, cache_key_blocks, preferred_element_type=jnp.float32
        )
        * factor
    )
    masked = jnp.where(live, scores, NEG)
    peak = jnp.max(masked, axis=-1)
    weights = jnp.where(live, jnp.exp(masked - peak[..., None]), 0.0)
    total = jnp.sum(weights, axis=-1)
    weighted = jnp.einsum(
        "tqgwj,tjgd->tqgwd",
        weights.astype(jnp.bfloat16),
        cache_value_blocks,
        preferred_element_type=jnp.float32,
    )
    part_top = peak.reshape(tokens, heads_here)
    part_total = total.reshape(tokens, heads_here)
    part_out = weighted.reshape(tokens, heads_here, HEAD_SIZE)
    n_ctx = lax.axis_size("ctx")
    all_rows = tokens * heads_here
    share = all_rows // n_ctx
    got_top, got_total, got_out = (
        lax.all_to_all(
            part_top.reshape(1, all_rows), "ctx", split_axis=1, concat_axis=0, tiled=True
        ),
        lax.all_to_all(
            part_total.reshape(1, all_rows), "ctx", split_axis=1, concat_axis=0, tiled=True
        ),
        lax.all_to_all(
            part_out.reshape(1, all_rows, HEAD_SIZE), "ctx", split_axis=1, concat_axis=0, tiled=True
        ),
    )
    summit = jnp.max(got_top, axis=0)
    rescale = jnp.exp(got_top - summit)
    merged = (
        summit,
        jnp.sum(got_total * rescale, axis=0),
        jnp.sum(got_out * rescale[..., None], axis=0),
    )
    first_row = lax.axis_index("ctx") * share
    row_ids = first_row + jnp.arange(share, dtype=jnp.int32)
    token_rows = row_ids // heads_here
    group_rows = row_ids % heads_here // group_width
    query_rows = lax.dynamic_slice_in_dim(
        sorted_queries.reshape(all_rows, HEAD_SIZE), first_row, share, 0
    )
    own = draft_rows(
        query_rows, group_rows, visible[token_rows], draft_key_lines, draft_value_lines, factor
    )
    final_top, final_total, final_out = combine(merged, own)
    finished = (final_out / final_total[:, None]).astype(jnp.bfloat16)
    attention = lax.all_gather(finished, "ctx", axis=0, tiled=True).reshape(
        tokens, heads_here * HEAD_SIZE
    )
    attention_split = attention.reshape(tenants, draft, -1)
    projected = jnp.dot(attention, out_weight, preferred_element_type=jnp.float32)
    out_delta = jnp.einsum(
        "tqh,thf->tqf", attention_split, out_signs, preferred_element_type=jnp.float32
    )
    projected = projected + (
        out_delta * (delta_scale[:, 0] * (QUERY_HEADS * HEAD_SIZE) ** (-0.5))[:, None, None]
    ).reshape(tokens, -1)
    summed_heads = lax.psum(projected.astype(jnp.bfloat16), "kv").astype(jnp.float32)
    hidden = residual[sort_order].astype(jnp.float32) + summed_heads
    squares = lax.psum(jnp.sum(hidden * hidden, axis=1), "ctx")
    normed = (hidden * lax.rsqrt(squares / D + EPS)[:, None] * norm_gain).astype(jnp.bfloat16)
    hidden_units = gate_weight.shape[1]
    piece = lax.all_gather(normed, "ctx", axis=1, tiled=True)
    size = piece.shape[1]
    split_piece = piece.reshape(tenants, draft, size)
    gate_base = jnp.dot(piece, gate_weight, preferred_element_type=jnp.float32)
    up_base = jnp.dot(piece, up_weight, preferred_element_type=jnp.float32)
    gate_delta = jnp.einsum(
        "tqf,tfh->tqh", split_piece, gate_signs, preferred_element_type=jnp.float32
    )
    up_delta = jnp.einsum("tqf,tfh->tqh", split_piece, up_signs, preferred_element_type=jnp.float32)
    gate = gate_base + (gate_delta * (delta_scale[:, 1] * D ** (-0.5))[:, None, None]).reshape(
        tokens, hidden_units
    )
    up_part = up_base + (up_delta * (delta_scale[:, 2] * D ** (-0.5))[:, None, None]).reshape(
        tokens, hidden_units
    )
    active = (jax.nn.silu(gate) * up_part).astype(jnp.bfloat16)
    active_split = active.reshape(tenants, draft, hidden_units)
    down_factor = delta_scale[:, 3] * FF ** (-0.5)
    features_here = residual.shape[1]
    base_part = lax.dot_general(
        down_weight, active, (((0,), (1,)), ((), ())), preferred_element_type=jnp.float32
    )
    delta_part = jnp.einsum(
        "thf,tqh->ftq", down_signs, active_split, preferred_element_type=jnp.float32
    )
    delta_part = delta_part * down_factor[None, :, None]
    lowered = lax.psum_scatter(
        base_part + delta_part.reshape(features_here * lax.axis_size("ctx"), tokens),
        "ctx",
        scatter_dimension=0,
        tiled=True,
    )
    lowered = lax.psum(lowered.astype(jnp.bfloat16), "kv").astype(jnp.float32)
    return (hidden + lowered.T).astype(jnp.bfloat16)[inverse]


def solution(mesh):
    return jax.shard_map(
        shards,
        mesh=mesh,
        in_specs=(
            P(None, "ctx"),
            P(None, "kv"),
            P(None, "kv"),
            P(None, "kv"),
            P(None, "ctx", "kv"),
            P(None, "ctx", "kv"),
            P(),
            P(),
            P(),
            P("kv", "ctx"),
            P(None, "kv", "ctx"),
            P("ctx"),
            P(None, ("kv", "ctx")),
            P(None, ("kv", "ctx")),
            P(("kv", "ctx"), None),
            P(None, None, ("kv", "ctx")),
            P(None, None, ("kv", "ctx")),
            P(None, ("kv", "ctx"), None),
            P(),
        ),
        out_specs=P(None, "ctx"),
        check_vma=False,
    )
```

profile of v0, /device:TPU:0, one launch (start us, length us, event | category | flops | bytes accessed | tf_op | source)
XLA Modules:
  0.0 308.4 jit_solution(11207596414709739598)
XLA Ops:
  6.5 2.8 sort.34
  9.4 0.9 gather_fusion.1
  10.4 0.3 reshape.250
  10.7 0.9 bitcast_reduce_fusion
  11.7 1.9 copy-done.3
  13.6 1.3 fusion.3
  14.9 0.8 all_to_all.38
  15.7 7.4 %all-to-all-start.2 = ((f32[1,16,128]{2,0,1:T(1,128)}), f32[1,16,128]{2,0,1:T(1,128)S(1)}, u32[]{:S(2)}, u32[]{:S(2)}) async-start(f32[1,16,128]{2,0,1:T(1,128)} %bitcast.17), calls=%async_computation.2 | async-start | bytes 16384 | tf_op jit(solution)/shard_map/all_to_all | solution.py:112
  23.1 1.1 reshape.251
  24.2 3.6 %fusion.9 = f32[2,32,4,8,128]{4,3,1,2,0:T(8,128)S(1)} fusion(f32[2,4,32,8,512]{4,3,2,1,0:T(8,128)} %copy-done.3, f32[2,32,4,8]{3,1,2,0:T(8,128)S(1)} %get-tuple-element.20, pred[2,512]{1,0:T(4,128)(4,1)S(1)} %broadcast_compare_fusion, bf16[2,512,4,128,1]{3,2,1,0,4:T(4,128)(2,1)} %bitcast.112), kind=kOutput, calls=%fused_computation.21 | convolution fusion | flops 273678336 | bytes 6300672 | tf_op jit(solution)/shard_map/tqgwj,tjgd->tqgwd/dot_general | solution.py:96
  27.9 0.7 all_to_all.35
  28.7 0.8 all-to-all-done.2
  29.4 5.2 %all-to-all-start.1 = ((f32[1,16,128]{2,0,1:T(1,128)}), f32[1,16,128]{2,0,1:T(1,128)S(1)}, u32[]{:S(2)}, u32[]{:S(2)}) async-start(f32[1,16,128]{2,0,1:T(1,128)} %bitcast.7), calls=%async_computation.1 | async-start | bytes 16384 | tf_op jit(solution)/shard_map/all_to_all | solution.py:109
  34.7 0.2 reshape.253
  35.0 1.1 copy.49
  36.1 5.0 %all-to-all-done.1 = f32[1,16,128]{2,0,1:T(1,128)S(1)} async-done(((f32[1,16,128]{2,0,1:T(1,128)}), f32[1,16,128]{2,0,1:T(1,128)S(1)}, u32[]{:S(2)}, u32[]{:S(2)}) %all-to-all-start.1) | async-done | bytes 8224 | tf_op jit(solution)/shard_map/all_to_all | solution.py:109
  41.1 3.7 %all-to-all-start = ((f32[1,2048,128]{2,0,1:T(1,128)}), f32[1,2048,128]{2,0,1:T(1,128)S(1)}, u32[]{:S(2)}, u32[]{:S(2)}) async-start(f32[1,2048,128]{2,0,1:T(1,128)} %bitcast.5), calls=%async_computation | async-start | bytes 2097152 | tf_op jit(solution)/shard_map/all_to_all | solution.py:115
  45.0 0.7 gather_fusion.5
  45.7 0.6 gather_fusion.2
  46.4 0.6 gather_fusion.3
  47.2 0.7 gather_fusion.4
  47.9 0.7 gather_fusion.6
  49.3 0.7 fusion.22
  50.1 17.5 %all-to-all-done = f32[1,2048,128]{2,0,1:T(1,128)S(1)} async-done(((f32[1,2048,128]{2,0,1:T(1,128)}), f32[1,2048,128]{2,0,1:T(1,128)S(1)}, u32[]{:S(2)}, u32[]{:S(2)}) %all-to-all-start) | async-done | bytes 1048608 | tf_op jit(solution)/shard_map/all_to_all | solution.py:115
  67.6 0.3 multiply_reduce_fusion
  68.1 24.0 %all_gather.6 = bf16[2048,128]{1,0:T(8,128)(2,1)S(1)} all-gather(bf16[128,128]{1,0:T(8,128)(2,1)S(1)} %divide_convert_fusion), channel_id=1, replica_groups=mesh['kv'=2,'ctx'=16] {'ctx'}, dimensions={0}, use_global_device_ids=true | all-gather | bytes 557056 | tf_op jit(solution)/shard_map/all_gather | solution.py:138
  92.6 5.1 %convolution_multiply_fusion.1 = f32[2,32,512]{2,1,0:T(8,128)S(1)} fusion(bf16[2,32,4096]{2,1,0:T(8,128)(2,1)S(1)} %reshape_reshape.9, bf16[2,4096,512]{2,1,0:T(8,128)(2,1)} %param.29, f32[2]{0:T(128)S(1)} %get-tuple-element.11), kind=kOutput, calls=%fused_computation.22 | convolution fusion | flops 268468224 | bytes 9043976 | tf_op jit(solution)/shard_map/tqh,thf->tqf/dot_general | solution.py:143
  97.6 1.5 fusion.16
  99.2 0.7 gather_fusion
  99.9 17.6 %all-reduce.3.cloned.1.call-done = bf16[64,512]{1,0:T(8,128)(2,1)} async-done(((bf16[64,512]{1,0:T(8,128)(2,1)}), bf16[64,512]{1,0:T(8,128)(2,1)}) %all-reduce.3.cloned.1.call-update) | async-done | bytes 65552 | tf_op jit(solution)/shard_map/psum | solution.py:149
  117.5 1.0 multiply_reduce_fusion.1
  118.5 32.7 %psum.22 = f32[64]{0:T(128)S(1)} all-reduce(f32[64]{0:T(128)S(1)} %multiply_reduce_fusion.1), channel_id=1, replica_groups=mesh['kv'=2,'ctx'=16] {'ctx'}, use_global_device_ids=true, to_apply=%region_10.11 | all-reduce | flops 64 | bytes 512 | tf_op jit(solution)/shard_map/psum | solution.py:151
  151.2 1.6 multiply_convert_fusion
  153.0 32.9 %all-gather.2.cloned.1.call-done = bf16[64,8192]{1,0:T(8,128)(2,1)} async-done(((bf16[64,512]{1,0:T(8,128)(2,1)}), bf16[64,8192]{1,0:T(8,128)(2,1)}) %all-gather.2.cloned.1.call-update) | async-done | bytes 1048592 | tf_op jit(solution)/shard_map/all_gather | solution.py:154
  185.9 9.1 %convolution_multiply_fusion.3 = f32[2,32,512]{2,1,0:T(8,128)S(1)} fusion(bf16[2,32,8192]{2,1,0:T(8,128)(2,1)} %bitcast.93, bf16[2,8192,512]{2,1,0:T(8,128)(2,1)} %param.34, f32[2]{0:T(128)S(1)} %get-tuple-element.10), kind=kOutput, calls=%fused_computation.27 | convolution fusion | flops 536903680 | bytes 17956872 | tf_op jit(solution)/shard_map/tqf,tfh->tqh/dot_general | solution.py:159
  195.1 8.8 %convolution_multiply_fusion.2 = f32[2,32,512]{2,1,0:T(8,128)S(1)} fusion(bf16[2,32,8192]{2,1,0:T(8,128)(2,1)S(1)} %bitcast.94, bf16[2,8192,512]{2,1,0:T(8,128)(2,1)} %param.35, f32[2]{0:T(128)S(1)} %get-tuple-element.12), kind=kOutput, calls=%fused_computation.24 | convolution fusion | flops 536903680 | bytes 17956872 | tf_op jit(solution)/shard_map/tqf,tfh->tqh/dot_general | solution.py:162
  204.0 1.6 convolution_add_fusion.2
  205.7 1.6 fusion.15
  207.5 1.2 slice-done.8
  208.7 1.4 slice-done.9
  210.1 3.0 convolution_multiply_fusion
  213.1 2.9 fusion
  216.1 2.0 sort.35
  218.1 59.5 %reduce-scatter.2.cloned.1.call-done = f32[512,64]{0,1:T(8,128)} async-done(((f32[8192,64]{0,1:T(8,128)}), f32[512,64]{0,1:T(8,128)}) %reduce-scatter.2.cloned.1.call-update) | async-done | bytes 131088 | tf_op jit(solution)/shard_map/reduce_scatter | solution.py:180
  277.7 1.5 convert_bitcast_fusion
  279.3 20.4 %all-reduce.5.cloned.1.call-done = bf16[64,512]{1,0:T(8,128)(2,1)} async-done(((bf16[64,512]{1,0:T(8,128)(2,1)}), bf16[64,512]{1,0:T(8,128)(2,1)}) %all-reduce.5.cloned.1.call-update) | async-done | bytes 65552 | tf_op jit(solution)/shard_map/psum | solution.py:186
  299.7 0.9 add_convert_fusion
  300.6 1.3 gather_fusion.7
  (91 shorter events, 3.0 us)
Async XLA Ops:
  6.5 2.8 copy-start
  6.5 3.8 %copy-start.9 = (bf16[2,512,512]{2,1,0:T(8,128)(2,1)S(1)}, bf16[2,512,512]{2,1,0:T(8,128)(2,1)}, u32[]{:S(2)}) copy-start(bf16[2,512,512]{2,1,0:T(8,128)(2,1)} %param.23) | copy-start | bytes 3145732
  6.5 4.1 %copy-start.14 = (s32[2]{0:T(128)S(1)}, s32[2]{0:T(128)}, u32[]{:S(2)}) copy-start(s32[2]{0:T(128)} %param.27) | copy-start | bytes 28
  10.7 12.3 %copy-start.10 = (bf16[2,512,512]{2,1,0:T(8,128)(2,1)S(1)}, bf16[2,512,512]{2,1,0:T(8,128)(2,1)}, u32[]{:S(2)}) copy-start(bf16[2,512,512]{2,1,0:T(8,128)(2,1)} %param.24) | copy-start | bytes 3145732
  11.6 1.9 copy-start.3
  15.7 13.8 %all-to-all-start.2 = ((f32[1,16,128]{2,0,1:T(1,128)}), f32[1,16,128]{2,0,1:T(1,128)S(1)}, u32[]{:S(2)}, u32[]{:S(2)}) async-start(f32[1,16,128]{2,0,1:T(1,128)} %bitcast.17), calls=%async_computation.2 | async-start | bytes 16384 | tf_op jit(solution)/shard_map/all_to_all | solution.py:112
  27.8 17.2 %copy-start.5 = (bf16[64,512]{1,0:T(8,128)(2,1)S(1)}, bf16[64,512]{1,0:T(8,128)(2,1)}, u32[]{:S(2)}) copy-start(bf16[64,512]{1,0:T(8,128)(2,1)} %param.21) | copy-start | bytes 196612
  27.8 17.9 %copy-start.8 = (s32[64,64]{1,0:T(8,128)S(1)}, s32[64,64]{1,0:T(8,128)}, u32[]{:S(2)}) copy-start(s32[64,64]{1,0:T(8,128)} %param.26) | copy-start | bytes 49156
  27.8 20.1 %copy-start.6 = (bf16[64,512]{1,0:T(8,128)(2,1)S(1)}, bf16[64,512]{1,0:T(8,128)(2,1)}, u32[]{:S(2)}) copy-start(bf16[64,512]{1,0:T(8,128)(2,1)} %param.22) | copy-start | bytes 196612
  27.8 20.8 %copy-start.12 = (f32[2,4]{1,0:T(2,128)S(1)}, f32[2,4]{1,0:T(2,128)}, u32[]{:S(2)}) copy-start(f32[2,4]{1,0:T(2,128)} %param.37) | copy-start | bytes 100
  29.4 11.7 %all-to-all-start.1 = ((f32[1,16,128]{2,0,1:T(1,128)}), f32[1,16,128]{2,0,1:T(1,128)S(1)}, u32[]{:S(2)}, u32[]{:S(2)}) async-start(f32[1,16,128]{2,0,1:T(1,128)} %bitcast.7), calls=%async_computation.1 | async-start | bytes 16384 | tf_op jit(solution)/shard_map/all_to_all | solution.py:109
  41.1 26.5 %all-to-all-start = ((f32[1,2048,128]{2,0,1:T(1,128)}), f32[1,2048,128]{2,0,1:T(1,128)S(1)}, u32[]{:S(2)}, u32[]{:S(2)}) async-start(f32[1,2048,128]{2,0,1:T(1,128)} %bitcast.5), calls=%async_computation | async-start | bytes 2097152 | tf_op jit(solution)/shard_map/all_to_all | solution.py:115
  44.8 72.7 %all-reduce.3.cloned.1.call-start = ((), (), s32[]{:S(2)}) async-start(), calls=%async_computation.4 | async-start | bytes 131072 | tf_op jit(solution)/shard_map/psum | solution.py:149
  92.5 5.1 %copy-start.4 = (bf16[4096,512]{1,0:T(8,128)(2,1)S(1)}, bf16[4096,512]{1,0:T(8,128)(2,1)}, u32[]{:S(2)}) copy-start(bf16[4096,512]{1,0:T(8,128)(2,1)} %param.28) | copy-start | bytes 12582916
  97.6 1.6 copy-start.7
  97.6 53.6 %copy-start.13 = (f32[512]{0:T(512)S(1)}, f32[512]{0:T(512)}, u32[]{:S(2)}) copy-start(f32[512]{0:T(512)} %param.30) | copy-start | bytes 6148
  99.1 86.8 %all-gather.2.cloned.1.call-start = ((), (), s32[]{:S(2)}) async-start(), calls=%async_computation.5 | async-start | bytes 1114112 | tf_op jit(solution)/shard_map/all_gather | solution.py:154
  152.8 124.9 %reduce-scatter.2.cloned.1.call-start = ((), (), s32[]{:S(2)}) async-start(), calls=%async_computation.6 | async-start | bytes 2228224 | tf_op jit(solution)/shard_map/reduce_scatter | solution.py:180
  185.9 9.2 %copy-start.2 = (bf16[64,8192]{1,0:T(8,128)(2,1)S(1)}, bf16[64,8192]{1,0:T(8,128)(2,1)}, u32[]{:S(2)}) copy-start(bf16[64,8192]{1,0:T(8,128)(2,1)} %all-gather.2.cloned.1.call-done) | copy-start | bytes 3145732
  185.9 18.1 %slice-start = ((s8[8388608]{0:T(1024)(128)(4,1)}), s8[4194304]{0:T(1024)(128)(4,1)S(1)}, s32[]{:S(2)}) async-start(s8[8388608]{0:T(1024)(128)(4,1)} %bitcast.95), calls=%async_computation.8 | async-start | bytes 8388608
  185.9 19.7 %slice-start.2 = ((s8[8388608]{0:T(1024)(128)(4,1)}), s8[4194304]{0:T(1024)(128)(4,1)S(1)}, s32[]{:S(2)}) async-start(s8[8388608]{0:T(1024)(128)(4,1)} %bitcast.97), calls=%async_computation.10 | async-start | bytes 8388608
  195.1 8.9 %slice-start.1 = ((s8[8388608]{0:T(1024)(128)(4,1)}), s8[4194304]{0:T(1024)(128)(4,1)S(1)}, s32[]{:S(2)}) async-start(s8[8388608]{0:T(1024)(128)(4,1)} %bitcast.95), calls=%async_computation.9 | async-start | bytes 8388608
  195.1 10.5 %slice-start.3 = ((s8[8388608]{0:T(1024)(128)(4,1)}), s8[4194304]{0:T(1024)(128)(4,1)S(1)}, s32[]{:S(2)}) async-start(s8[8388608]{0:T(1024)(128)(4,1)} %bitcast.97), calls=%async_computation.11 | async-start | bytes 8388608
  204.0 3.2 %slice-start.6 = ((s8[16777216]{0:T(1024)(128)(4,1)}), s8[4194304]{0:T(1024)(128)(4,1)S(1)}, s32[]{:S(2)}) async-start(s8[16777216]{0:T(1024)(128)(4,1)} %bitcast.102), calls=%async_computation.14 | async-start | bytes 8388608
  204.0 3.5 %slice-start.7 = ((s8[16777216]{0:T(1024)(128)(4,1)}), s8[4194304]{0:T(1024)(128)(4,1)S(1)}, s32[]{:S(2)}) async-start(s8[16777216]{0:T(1024)(128)(4,1)} %bitcast.102), calls=%async_computation.15 | async-start | bytes 8388608
  204.0 4.6 %slice-start.8 = ((s8[16777216]{0:T(1024)(128)(4,1)}), s8[4194304]{0:T(1024)(128)(4,1)S(1)}, s32[]{:S(2)}) async-start(s8[16777216]{0:T(1024)(128)(4,1)} %bitcast.102), calls=%async_computation.16 | async-start | bytes 8388608
  205.6 4.4 %slice-start.9 = ((s8[16777216]{0:T(1024)(128)(4,1)}), s8[4194304]{0:T(1024)(128)(4,1)S(1)}, s32[]{:S(2)}) async-start(s8[16777216]{0:T(1024)(128)(4,1)} %bitcast.102), calls=%async_computation.17 | async-start | bytes 8388608
  205.6 7.4 %slice-start.4 = ((s8[8388608]{0:T(1024)(128)(4,1)}), s8[4194304]{0:T(1024)(128)(4,1)S(1)}, s32[]{:S(2)}) async-start(s8[8388608]{0:T(1024)(128)(4,1)} %bitcast.99), calls=%async_computation.12 | async-start | bytes 8388608
  210.1 3.0 slice-start.5
  213.1 86.6 %copy-start.11 = (bf16[64,512]{1,0:T(8,128)(2,1)S(1)}, bf16[64,512]{1,0:T(8,128)(2,1)}, u32[]{:S(2)}) copy-start(bf16[64,512]{1,0:T(8,128)(2,1)} %all-reduce.3.cloned.1.call-done) | copy-start | bytes 196612
  213.1 88.8 %copy-start.1 = (bf16[64,4096]{1,0:T(8,128)(2,1)S(1)}, bf16[64,4096]{1,0:T(8,128)(2,1)}, u32[]{:S(2)}) copy-start(bf16[64,4096]{1,0:T(8,128)(2,1)} %param.20) | copy-start | bytes 1572868
  216.1 83.7 %all-reduce.5.cloned.1.call-start = ((), (), s32[]{:S(2)}) async-start(), calls=%async_computation.7 | async-start | bytes 131072 | tf_op jit(solution)/shard_map/psum | solution.py:186
Sparse Core Ops, SparseCore 0:
  99.3 18.2 all-reduce.2
  152.9 32.9 all-gather.1
  216.2 61.4 reduce-scatter.1
  279.8 19.8 all-reduce.4
where the time goes:
time: 309 us; the launch traced here: 308 us
  waiting for transfers between devices  154 us (50%)
  blocking collectives  56.7 us (18%)
  matrix products  39 us (13%)
  starting transfers between devices  16.6 us (5%)
  local copies, waits for them, and re-layouts  16.5 us (5%)
  between operations  13.7 us (4%)
  other arithmetic  12.1 us (4%)
    reduce_scatter x1, waiting for transfers between devices, shards(): lax.psum_scatter(base_part + delta_part.reshape(features_here * lax.axis_...  59.5 us
    all_gather x1, waiting for transfers between devices, shards(): piece = lax.all_gather(normed, 'ctx', axis=1, tiled=True)  32.9 us
    psum x1, blocking collectives, shards(): squares = lax.psum(jnp.sum(hidden * hidden, axis=1), 'ctx')  32.7 us
    all_gather x1, blocking collectives, shards(): lax.all_gather(finished, 'ctx', axis=0, tiled=True)  24 us
    psum x1, waiting for transfers between devices, shards(): lowered = lax.psum(lowered.astype(jnp.bfloat16), 'kv').astype(jnp.float32)  20.4 us
    psum x1, waiting for transfers between devices, shards(): lax.psum(projected.astype(jnp.bfloat16), 'kv').astype(jnp.float32)  17.6 us
    all_to_all x1, waiting for transfers between devices, shards(): lax.all_to_all(part_out.reshape(1, all_rows, HEAD_SIZE), 'ctx', split_axi...  17.5 us
    dot_general x1, matrix products, shards(): jnp.einsum('tqf,tfh->tqh', split_piece, gate_signs, preferred_element_typ...  9.14 us
  transfers between devices with their start and end apart: 7, of which 7 were waited for; matrix products, arithmetic and copies ran while one was open for 5% of the time, Pallas kernels for 0%

commit v1 on v0

--- a/solution.py
+++ b/solution.py
@@ -148,7 +148,7 @@
     ).reshape(tokens, -1)
     summed_heads = lax.psum(projected.astype(jnp.bfloat16), "kv").astype(jnp.float32)
     hidden = residual[sort_order].astype(jnp.float32) + summed_heads
-    squares = lax.psum(jnp.sum(hidden * hidden, axis=1), "ctx")
+    squares = jnp.sum(lax.all_gather(jnp.sum(hidden * hidden, axis=1), "ctx"), axis=0)
     normed = (hidden * lax.rsqrt(squares / D + EPS)[:, None] * norm_gain).astype(jnp.bfloat16)
     hidden_units = gate_weight.shape[1]
     piece = lax.all_gather(normed, "ctx", axis=1, tiled=True)

time: 309 us -> 309 us (level)
    psum x1 -> x0, blocking collectives: 32.7 us -> none  [shards(): squares = lax.psum(jnp.sum(hidden * hidden, axis=1), 'ctx')]
    unnamed x0 -> x1, blocking collectives: none -> 32.7 us
where the time goes in v1:
time: 309 us
  waiting for transfers between devices  152 us (49%)
  blocking collectives  56.7 us (18%)
  matrix products  39 us (13%)
  local copies, waits for them, and re-layouts  17.5 us (6%)
  starting transfers between devices  16.6 us (5%)
  between operations  14.4 us (5%)
  other arithmetic  12.1 us (4%)
    reduce_scatter x1, waiting for transfers between devices, shards(): lax.psum_scatter(base_part + delta_part.reshape(features_here * lax.axis_...  59.5 us
    all_gather x1, waiting for transfers between devices, shards(): piece = lax.all_gather(normed, 'ctx', axis=1, tiled=True)  32.9 us
    unnamed x1, blocking collectives  32.7 us
    all_gather x1, blocking collectives, shards(): lax.all_gather(finished, 'ctx', axis=0, tiled=True)  24 us
    psum x1, waiting for transfers between devices, shards(): lowered = lax.psum(lowered.astype(jnp.bfloat16), 'kv').astype(jnp.float32)  20.4 us
    all_to_all x1, waiting for transfers between devices, shards(): lax.all_to_all(part_out.reshape(1, all_rows, HEAD_SIZE), 'ctx', split_axi...  17.5 us
    psum x1, waiting for transfers between devices, shards(): lax.psum(projected.astype(jnp.bfloat16), 'kv').astype(jnp.float32)  16.2 us
    dot_general x1, matrix products, shards(): jnp.einsum('tqf,tfh->tqh', split_piece, gate_signs, preferred_element_typ...  9.14 us
  transfers between devices with their start and end apart: 7, of which 7 were waited for; matrix products, arithmetic and copies ran while one was open for 5% of the time, Pallas kernels for 0%

profile of v1, /device:TPU:0, one launch (start us, length us, event | category | flops | bytes accessed | tf_op | source)
XLA Modules:
  0.0 308.8 jit_solution(13892788078501685625)
XLA Ops:
  6.5 2.8 sort.34
  9.4 0.9 gather_fusion.1
  10.4 0.3 reshape.254
  10.7 0.9 bitcast_reduce_fusion
  11.7 1.9 copy-done.3
  13.6 1.3 fusion.3
  14.9 0.8 all_to_all.38
  15.7 7.4 %all-to-all-start.2 = ((f32[1,16,128]{2,0,1:T(1,128)}), f32[1,16,128]{2,0,1:T(1,128)S(1)}, u32[]{:S(2)}, u32[]{:S(2)}) async-start(f32[1,16,128]{2,0,1:T(1,128)} %bitcast.17), calls=%async_computation.2 | async-start | bytes 16384 | tf_op jit(solution)/shard_map/all_to_all | solution.py:112
  23.1 1.1 reshape.255
  24.2 3.6 %fusion.9 = f32[2,32,4,8,128]{4,3,1,2,0:T(8,128)S(1)} fusion(f32[2,4,32,8,512]{4,3,2,1,0:T(8,128)} %copy-done.3, f32[2,32,4,8]{3,1,2,0:T(8,128)S(1)} %get-tuple-element.20, pred[2,512]{1,0:T(4,128)(4,1)S(1)} %broadcast_compare_fusion, bf16[2,512,4,128,1]{3,2,1,0,4:T(4,128)(2,1)} %bitcast.113), kind=kOutput, calls=%fused_computation.21 | convolution fusion | flops 273678336 | bytes 6300672 | tf_op jit(solution)/shard_map/tqgwj,tjgd->tqgwd/dot_general | solution.py:96
  27.9 0.7 all_to_all.35
  28.7 0.8 all-to-all-done.2
  29.4 5.2 %all-to-all-start.1 = ((f32[1,16,128]{2,0,1:T(1,128)}), f32[1,16,128]{2,0,1:T(1,128)S(1)}, u32[]{:S(2)}, u32[]{:S(2)}) async-start(f32[1,16,128]{2,0,1:T(1,128)} %bitcast.7), calls=%async_computation.1 | async-start | bytes 16384 | tf_op jit(solution)/shard_map/all_to_all | solution.py:109
  35.0 1.1 copy.63
  36.1 5.0 %all-to-all-done.1 = f32[1,16,128]{2,0,1:T(1,128)S(1)} async-done(((f32[1,16,128]{2,0,1:T(1,128)}), f32[1,16,128]{2,0,1:T(1,128)S(1)}, u32[]{:S(2)}, u32[]{:S(2)}) %all-to-all-start.1) | async-done | bytes 8224 | tf_op jit(solution)/shard_map/all_to_all | solution.py:109
  41.1 3.7 %all-to-all-start = ((f32[1,2048,128]{2,0,1:T(1,128)}), f32[1,2048,128]{2,0,1:T(1,128)S(1)}, u32[]{:S(2)}, u32[]{:S(2)}) async-start(f32[1,2048,128]{2,0,1:T(1,128)} %bitcast.5), calls=%async_computation | async-start | bytes 2097152 | tf_op jit(solution)/shard_map/all_to_all | solution.py:115
  45.0 0.7 gather_fusion.5
  45.7 0.6 gather_fusion.2
  46.4 0.6 gather_fusion.3
  47.2 0.7 gather_fusion.4
  47.9 0.7 gather_fusion.6
  49.3 0.7 fusion.22
  50.1 17.5 %all-to-all-done = f32[1,2048,128]{2,0,1:T(1,128)S(1)} async-done(((f32[1,2048,128]{2,0,1:T(1,128)}), f32[1,2048,128]{2,0,1:T(1,128)S(1)}, u32[]{:S(2)}, u32[]{:S(2)}) %all-to-all-start) | async-done | bytes 1048608 | tf_op jit(solution)/shard_map/all_to_all | solution.py:115
  67.6 0.3 multiply_reduce_fusion
  68.1 24.0 %all_gather.12 = bf16[2048,128]{1,0:T(8,128)(2,1)S(1)} all-gather(bf16[128,128]{1,0:T(8,128)(2,1)S(1)} %divide_convert_fusion), channel_id=1, replica_groups=mesh['kv'=2,'ctx'=16] {'ctx'}, dimensions={0}, use_global_device_ids=true | all-gather | bytes 557056 | tf_op jit(solution)/shard_map/all_gather | solution.py:138
  92.6 5.1 %convolution_multiply_fusion.1 = f32[2,32,512]{2,1,0:T(8,128)S(1)} fusion(bf16[2,32,4096]{2,1,0:T(8,128)(2,1)S(1)} %reshape_reshape.9, bf16[2,4096,512]{2,1,0:T(8,128)(2,1)} %param.29, f32[2]{0:T(128)S(1)} %get-tuple-element.11), kind=kOutput, calls=%fused_computation.22 | convolution fusion | flops 268468224 | bytes 9043976 | tf_op jit(solution)/shard_map/tqh,thf->tqf/dot_general | solution.py:143
  97.7 1.5 fusion.16
  99.2 0.7 gather_fusion
  99.9 0.7 dynamic-slice
  101.3 16.2 %all-reduce.4.cloned.1.call-done = bf16[64,512]{1,0:T(8,128)(2,1)} async-done(((bf16[64,512]{1,0:T(8,128)(2,1)}), bf16[64,512]{1,0:T(8,128)(2,1)}) %all-reduce.4.cloned.1.call-update) | async-done | bytes 65552 | tf_op jit(solution)/shard_map/psum | solution.py:149
  117.5 1.0 multiply_reduce_fusion.1
  118.8 32.7 %all-reduce = f32[1024]{0:T(1024)S(1)} all-reduce(f32[1024]{0:T(1024)S(1)} %dynamic-update-slice), channel_id=2, replica_groups=mesh['kv'=2,'ctx'=16] {'ctx'}, use_global_device_ids=true, to_apply=%add | all-reduce | flops 1024 | bytes 8192
  151.5 1.6 multiply_convert_fusion
  153.4 32.9 %all-gather.3.cloned.1.call-done = bf16[64,8192]{1,0:T(8,128)(2,1)} async-done(((bf16[64,512]{1,0:T(8,128)(2,1)}), bf16[64,8192]{1,0:T(8,128)(2,1)}) %all-gather.3.cloned.1.call-update) | async-done | bytes 1048592 | tf_op jit(solution)/shard_map/all_gather | solution.py:154
  186.2 9.1 %convolution_multiply_fusion.3 = f32[2,32,512]{2,1,0:T(8,128)S(1)} fusion(bf16[2,32,8192]{2,1,0:T(8,128)(2,1)} %bitcast.94, bf16[2,8192,512]{2,1,0:T(8,128)(2,1)} %param.34, f32[2]{0:T(128)S(1)} %get-tuple-element.10), kind=kOutput, calls=%fused_computation.27 | convolution fusion | flops 536903680 | bytes 17956872 | tf_op jit(solution)/shard_map/tqf,tfh->tqh/dot_general | solution.py:159
  195.5 8.8 %convolution_multiply_fusion.2 = f32[2,32,512]{2,1,0:T(8,128)S(1)} fusion(bf16[2,32,8192]{2,1,0:T(8,128)(2,1)S(1)} %bitcast.95, bf16[2,8192,512]{2,1,0:T(8,128)(2,1)} %param.35, f32[2]{0:T(128)S(1)} %get-tuple-element.12), kind=kOutput, calls=%fused_computation.24 | convolution fusion | flops 536903680 | bytes 17956872 | tf_op jit(solution)/shard_map/tqf,tfh->tqh/dot_general | solution.py:162
  204.4 1.6 convolution_add_fusion.2
  206.0 1.6 fusion.15
  207.8 1.2 slice-done.8
  209.0 1.4 slice-done.9
  210.4 3.0 convolution_multiply_fusion
  213.4 2.9 fusion
  216.5 2.0 sort.35
  218.5 59.5 %reduce-scatter.2.cloned.1.call-done = f32[512,64]{0,1:T(8,128)} async-done(((f32[8192,64]{0,1:T(8,128)}), f32[512,64]{0,1:T(8,128)}) %reduce-scatter.2.cloned.1.call-update) | async-done | bytes 131088 | tf_op jit(solution)/shard_map/reduce_scatter | solution.py:180
  278.0 1.5 convert_bitcast_fusion
  279.6 20.4 %all-reduce.6.cloned.1.call-done = bf16[64,512]{1,0:T(8,128)(2,1)} async-done(((bf16[64,512]{1,0:T(8,128)(2,1)}), bf16[64,512]{1,0:T(8,128)(2,1)}) %all-reduce.6.cloned.1.call-update) | async-done | bytes 65552 | tf_op jit(solution)/shard_map/psum | solution.py:186
  300.1 0.9 add_convert_fusion
  300.9 1.3 gather_fusion.7
  (98 shorter events, 3.6 us)
Async XLA Ops:
  6.5 2.8 copy-start
  6.5 3.8 %copy-start.9 = (bf16[2,512,512]{2,1,0:T(8,128)(2,1)S(1)}, bf16[2,512,512]{2,1,0:T(8,128)(2,1)}, u32[]{:S(2)}) copy-start(bf16[2,512,512]{2,1,0:T(8,128)(2,1)} %param.23) | copy-start | bytes 3145732
  6.5 4.1 %copy-start.14 = (s32[2]{0:T(128)S(1)}, s32[2]{0:T(128)}, u32[]{:S(2)}) copy-start(s32[2]{0:T(128)} %param.27) | copy-start | bytes 28
  10.7 12.3 %copy-start.10 = (bf16[2,512,512]{2,1,0:T(8,128)(2,1)S(1)}, bf16[2,512,512]{2,1,0:T(8,128)(2,1)}, u32[]{:S(2)}) copy-start(bf16[2,512,512]{2,1,0:T(8,128)(2,1)} %param.24) | copy-start | bytes 3145732
  11.7 1.9 copy-start.3
  15.7 13.8 %all-to-all-start.2 = ((f32[1,16,128]{2,0,1:T(1,128)}), f32[1,16,128]{2,0,1:T(1,128)S(1)}, u32[]{:S(2)}, u32[]{:S(2)}) async-start(f32[1,16,128]{2,0,1:T(1,128)} %bitcast.17), calls=%async_computation.2 | async-start | bytes 16384 | tf_op jit(solution)/shard_map/all_to_all | solution.py:112
  27.8 17.2 %copy-start.5 = (bf16[64,512]{1,0:T(8,128)(2,1)S(1)}, bf16[64,512]{1,0:T(8,128)(2,1)}, u32[]{:S(2)}) copy-start(bf16[64,512]{1,0:T(8,128)(2,1)} %param.21) | copy-start | bytes 196612
  27.8 17.9 %copy-start.8 = (s32[64,64]{1,0:T(8,128)S(1)}, s32[64,64]{1,0:T(8,128)}, u32[]{:S(2)}) copy-start(s32[64,64]{1,0:T(8,128)} %param.26) | copy-start | bytes 49156
  27.8 20.1 %copy-start.6 = (bf16[64,512]{1,0:T(8,128)(2,1)S(1)}, bf16[64,512]{1,0:T(8,128)(2,1)}, u32[]{:S(2)}) copy-start(bf16[64,512]{1,0:T(8,128)(2,1)} %param.22) | copy-start | bytes 196612
  27.8 20.8 %copy-start.12 = (f32[2,4]{1,0:T(2,128)S(1)}, f32[2,4]{1,0:T(2,128)}, u32[]{:S(2)}) copy-start(f32[2,4]{1,0:T(2,128)} %param.37) | copy-start | bytes 100
  29.4 11.7 %all-to-all-start.1 = ((f32[1,16,128]{2,0,1:T(1,128)}), f32[1,16,128]{2,0,1:T(1,128)S(1)}, u32[]{:S(2)}, u32[]{:S(2)}) async-start(f32[1,16,128]{2,0,1:T(1,128)} %bitcast.7), calls=%async_computation.1 | async-start | bytes 16384 | tf_op jit(solution)/shard_map/all_to_all | solution.py:109
  41.1 26.5 %all-to-all-start = ((f32[1,2048,128]{2,0,1:T(1,128)}), f32[1,2048,128]{2,0,1:T(1,128)S(1)}, u32[]{:S(2)}, u32[]{:S(2)}) async-start(f32[1,2048,128]{2,0,1:T(1,128)} %bitcast.5), calls=%async_computation | async-start | bytes 2097152 | tf_op jit(solution)/shard_map/all_to_all | solution.py:115
  44.8 72.7 %all-reduce.4.cloned.1.call-start = ((), (), s32[]{:S(2)}) async-start(), calls=%async_computation.4 | async-start | bytes 131072 | tf_op jit(solution)/shard_map/psum | solution.py:149
  92.5 5.1 %copy-start.4 = (bf16[4096,512]{1,0:T(8,128)(2,1)S(1)}, bf16[4096,512]{1,0:T(8,128)(2,1)}, u32[]{:S(2)}) copy-start(bf16[4096,512]{1,0:T(8,128)(2,1)} %param.28) | copy-start | bytes 12582916
  97.6 1.6 copy-start.7
  97.6 2.3 copy-start.15
  97.6 53.9 %copy-start.13 = (f32[512]{0:T(512)S(1)}, f32[512]{0:T(512)}, u32[]{:S(2)}) copy-start(f32[512]{0:T(512)} %param.30) | copy-start | bytes 6148
  99.1 87.1 %all-gather.3.cloned.1.call-start = ((), (), s32[]{:S(2)}) async-start(), calls=%async_computation.5 | async-start | bytes 1114112 | tf_op jit(solution)/shard_map/all_gather | solution.py:154
  153.1 124.9 %reduce-scatter.2.cloned.1.call-start = ((), (), s32[]{:S(2)}) async-start(), calls=%async_computation.6 | async-start | bytes 2228224 | tf_op jit(solution)/shard_map/reduce_scatter | solution.py:180
  186.2 9.2 %copy-start.2 = (bf16[64,8192]{1,0:T(8,128)(2,1)S(1)}, bf16[64,8192]{1,0:T(8,128)(2,1)}, u32[]{:S(2)}) copy-start(bf16[64,8192]{1,0:T(8,128)(2,1)} %all-gather.3.cloned.1.call-done) | copy-start | bytes 3145732
  186.2 18.1 %slice-start = ((s8[8388608]{0:T(1024)(128)(4,1)}), s8[4194304]{0:T(1024)(128)(4,1)S(1)}, s32[]{:S(2)}) async-start(s8[8388608]{0:T(1024)(128)(4,1)} %bitcast.96), calls=%async_computation.8 | async-start | bytes 8388608
  186.2 19.7 %slice-start.2 = ((s8[8388608]{0:T(1024)(128)(4,1)}), s8[4194304]{0:T(1024)(128)(4,1)S(1)}, s32[]{:S(2)}) async-start(s8[8388608]{0:T(1024)(128)(4,1)} %bitcast.98), calls=%async_computation.10 | async-start | bytes 8388608
  195.4 8.9 %slice-start.1 = ((s8[8388608]{0:T(1024)(128)(4,1)}), s8[4194304]{0:T(1024)(128)(4,1)S(1)}, s32[]{:S(2)}) async-start(s8[8388608]{0:T(1024)(128)(4,1)} %bitcast.96), calls=%async_computation.9 | async-start | bytes 8388608
  195.4 10.5 %slice-start.3 = ((s8[8388608]{0:T(1024)(128)(4,1)}), s8[4194304]{0:T(1024)(128)(4,1)S(1)}, s32[]{:S(2)}) async-start(s8[8388608]{0:T(1024)(128)(4,1)} %bitcast.98), calls=%async_computation.11 | async-start | bytes 8388608
  204.3 3.2 %slice-start.6 = ((s8[16777216]{0:T(1024)(128)(4,1)}), s8[4194304]{0:T(1024)(128)(4,1)S(1)}, s32[]{:S(2)}) async-start(s8[16777216]{0:T(1024)(128)(4,1)} %bitcast.103), calls=%async_computation.14 | async-start | bytes 8388608
  204.4 3.5 %slice-start.7 = ((s8[16777216]{0:T(1024)(128)(4,1)}), s8[4194304]{0:T(1024)(128)(4,1)S(1)}, s32[]{:S(2)}) async-start(s8[16777216]{0:T(1024)(128)(4,1)} %bitcast.103), calls=%async_computation.15 | async-start | bytes 8388608
  204.4 4.6 %slice-start.8 = ((s8[16777216]{0:T(1024)(128)(4,1)}), s8[4194304]{0:T(1024)(128)(4,1)S(1)}, s32[]{:S(2)}) async-start(s8[16777216]{0:T(1024)(128)(4,1)} %bitcast.103), calls=%async_computation.16 | async-start | bytes 8388608
  206.0 4.4 %slice-start.9 = ((s8[16777216]{0:T(1024)(128)(4,1)}), s8[4194304]{0:T(1024)(128)(4,1)S(1)}, s32[]{:S(2)}) async-start(s8[16777216]{0:T(1024)(128)(4,1)} %bitcast.103), calls=%async_computation.17 | async-start | bytes 8388608
  206.0 7.4 %slice-start.4 = ((s8[8388608]{0:T(1024)(128)(4,1)}), s8[4194304]{0:T(1024)(128)(4,1)S(1)}, s32[]{:S(2)}) async-start(s8[8388608]{0:T(1024)(128)(4,1)} %bitcast.100), calls=%async_computation.12 | async-start | bytes 8388608
  210.4 3.0 slice-start.5
  213.4 86.6 %copy-start.11 = (bf16[64,512]{1,0:T(8,128)(2,1)S(1)}, bf16[64,512]{1,0:T(8,128)(2,1)}, u32[]{:S(2)}) copy-start(bf16[64,512]{1,0:T(8,128)(2,1)} %all-reduce.4.cloned.1.call-done) | copy-start | bytes 196612
  213.4 88.8 %copy-start.1 = (bf16[64,4096]{1,0:T(8,128)(2,1)S(1)}, bf16[64,4096]{1,0:T(8,128)(2,1)}, u32[]{:S(2)}) copy-start(bf16[64,4096]{1,0:T(8,128)(2,1)} %param.20) | copy-start | bytes 1572868
  216.4 83.7 %all-reduce.6.cloned.1.call-start = ((), (), s32[]{:S(2)}) async-start(), calls=%async_computation.7 | async-start | bytes 131072 | tf_op jit(solution)/shard_map/psum | solution.py:186
Sparse Core Ops, SparseCore 0:
  99.3 18.2 all-reduce.3
  153.2 32.9 all-gather.2
  216.5 61.4 reduce-scatter.1
  280.1 19.8 all-reduce.5
